TPU v7x, 256 devices: a whole 4x4x8 slice. The times are simulated.
256 devices in a mesh: param: 64 (over x, z, y_hi), sensor: 4 (over y_lo, core).
Axes of the slice: x: 4, y: 4 (y_hi: 2, y_lo: 2; y = y_hi * 2 + y_lo), z: 8, core: 2. Of those that a mesh axis runs over, the one named last changes fastest.
Arguments:
- readings: bfloat16 [64, 600, 128], P('param', 'sensor'), may hold values from -6 to 6
- spectra: bfloat16 [2, 65, 600, 8192], P(None, None, 'sensor', 'param'), may hold values from -0.0625 to 0.0625
- stiffness: float32 [8192], P('param'), may hold values from 0.04 to 0.24
Outputs:
- hessian_panel: float32 [64, 600, 128], P('param', 'sensor')
All inputs are finite; a program needn't handle non-finite values.
Results may differ from a plain program's by a relative error of at most 0.0025.
Values may be sent and summed in bfloat16 or wider, within the bound.
No kernel may reach another device: no remote copies, remote signals or barrier semaphores. Data moves between devices by JAX's collectives and lax.ppermute only.
A program may use at most 128 MiB of HBM per device.

v0:
```python
import math
import jax
import jax.numpy as jnp
from jax import lax
from jax.sharding import PartitionSpec as P

STEPS = 64
GY = 64
NCOL = 128


def with_halo(block, sides, width):
    for axis, dim in sides:
        count = lax.axis_size(axis)
        forward = [(i, i + 1) for i in range(count - 1)]
        backward = [(target, source) for source, target in forward]
        low = lax.ppermute(
            lax.slice_in_dim(block, block.shape[dim] - width, None, axis=dim), axis, forward
        )
        high = lax.ppermute(lax.slice_in_dim(block, 0, width, axis=dim), axis, backward)
        block = jnp.concatenate([low, block, high], axis=dim)
    return block


def angles(bins, times):
    prod = bins[:, None] * times[None, :] % (2 * STEPS)
    return prod.astype(jnp.float32) * (2.0 * math.pi / (2 * STEPS))


def accumulate(loop_carry, piece):
    count = piece.shape[0]
    bins = jnp.arange(STEPS + 1, dtype=jnp.int32)
    times = jnp.arange(count, dtype=jnp.int32)
    phase_angle = angles(bins, times)
    scale_factor = 1.0 / math.sqrt(STEPS)
    value_entries = piece.astype(jnp.float32)
    hessian_product = lax.Precision.HIGHEST
    real_part = jnp.einsum(
        "uo,ojm->ujm", jnp.cos(phase_angle) * scale_factor, value_entries, precision=hessian_product
    )
    imaginary_part = loop_carry[1] - jnp.einsum(
        "uo,ojm->ujm", jnp.sin(phase_angle) * scale_factor, value_entries, precision=hessian_product
    )
    return (real_part, imaginary_part)


def inverse_rows(real_part, imaginary_part, count):
    bins = jnp.arange(STEPS + 1, dtype=jnp.int32)
    times = jnp.arange(count, dtype=jnp.int32)
    phase_angle = angles(bins, times)
    weight = jnp.where((bins == 0) | (bins == STEPS), 1.0, 2.0).astype(jnp.float32)[:, None]
    scale_factor = 1.0 / math.sqrt(STEPS)
    hessian_product = lax.Precision.HIGHEST
    cosine_inverse = (jnp.cos(phase_angle) * weight * scale_factor).T
    sine_inverse = (jnp.sin(phase_angle) * weight * scale_factor).T
    return jnp.einsum(
        "ni,ilj->nlj", cosine_inverse, real_part, precision=hessian_product
    ) - jnp.einsum("ni,ilj->nlj", sine_inverse, imaginary_part, precision=hessian_product)


def sweep_once(grid, coeff):
    padded = with_halo(grid.astype(jnp.bfloat16), (("param", 1),), 1).astype(grid.dtype)
    sides = jnp.pad(grid, ((0, 0), (0, 0), (1, 1), (0, 0)))
    beside_all = padded[:, :-2] + padded[:, 2:] + sides[:, :, :-2] + sides[:, :, 2:]
    return grid + coeff * (beside_all - 4.0 * grid)


def shards(readings, spectra, stiffness):
    sens_rows = readings.shape[1]
    points = spectra.shape[3]
    rows_here = points // GY
    empty_data = jnp.zeros((STEPS + 1, sens_rows, NCOL), jnp.float32)
    data_re, data_im = accumulate(
        (empty_data, empty_data), lax.all_gather(readings, "param", axis=0, tiled=True)
    )
    data_re = data_re.astype(jnp.bfloat16)
    data_im = data_im.astype(jnp.bfloat16)
    spectrum_real = spectra[0]
    spectrum_imaginary = spectra[1]
    f32 = jnp.float32
    adj_re = jnp.einsum(
        "ksm,ksc->kmc", spectrum_real, data_re, preferred_element_type=f32
    ) + jnp.einsum("ksm,ksc->kmc", spectrum_imaginary, data_im, preferred_element_type=f32)
    adj_im = jnp.einsum(
        "ksm,ksc->kmc", spectrum_real, data_im, preferred_element_type=f32
    ) - jnp.einsum("ksm,ksc->kmc", spectrum_imaginary, data_re, preferred_element_type=f32)
    field = inverse_rows(adj_re, adj_im, STEPS)
    grid = field.reshape(STEPS, rows_here, GY, NCOL)
    coeff = stiffness.reshape(rows_here, GY)[None, :, :, None]
    empty_model = jnp.zeros((STEPS + 1, points, NCOL), jnp.float32)
    grid = lax.psum(grid, "sensor")
    for sweep in range(2):
        grid = sweep_once(grid, coeff)
    model_re, model_im = accumulate((empty_model, empty_model), grid.reshape(STEPS, points, NCOL))
    model_re = model_re.astype(jnp.bfloat16)
    model_im = model_im.astype(jnp.bfloat16)
    out_re = jnp.einsum(
        "ksm,kmc->ksc", spectrum_real, model_re, preferred_element_type=f32
    ) - jnp.einsum("ksm,kmc->ksc", spectrum_imaginary, model_im, preferred_element_type=f32)
    out_im = jnp.einsum(
        "ksm,kmc->ksc", spectrum_real, model_im, preferred_element_type=f32
    ) + jnp.einsum("ksm,kmc->ksc", spectrum_imaginary, model_re, preferred_element_type=f32)
    return lax.psum_scatter(
        inverse_rows(out_re, out_im, readings.shape[0] * lax.axis_size("param")),
        "param",
        scatter_dimension=0,
        tiled=True,
    )


def solution(mesh):
    return jax.shard_map(
        shards,
        mesh=mesh,
        in_specs=(P("param", "sensor", None), P(None, None, "sensor", "param"), P("param")),
        out_specs=P("param", "sensor", None),
        check_vma=False,
    )
```

profile of v0, /device:TPU:8, one launch (start us, length us, event | category | flops | bytes accessed | tf_op | source)
XLA Modules:
  0.0 807.7 jit_solution(7636657847180767540)
XLA Ops:
  6.5 0.7 all-gather.2.cloned.1.call-update
  7.3 0.0 all-reduce.5.cloned.1.call-start
  7.3 10.1 %fusion.120 = (bf16[1,65,150,128]{3,0,2,1:T(2,128)(2,1)S(1)}, bf16[1,65,150,128]{3,0,2,1:T(2,128)(2,1)S(1)}) fusion(bf16[2,65,150,128]{3,0,2,1:T(2,128)(2,1)} %param.4), kind=kLoop, calls=%fused_computation.126 | loop fusion | bytes 9984000 | tf_op jit(solution)/shard_map/slice | solution.py:79
  17.5 2.7 copy_bitcast_fusion
  20.2 112.0 %all-gather.2.cloned.1.call-done = bf16[64,150,128]{2,1,0:T(8,128)(2,1)} async-done(((bf16[1,150,128]{2,1,0:T(8,128)(2,1)}), bf16[64,150,128]{2,1,0:T(8,128)(2,1)}) %all-gather.2.cloned.1.call-update) | async-done | bytes 2457616 | tf_op jit(solution)/shard_map/all_gather | solution.py:74
  132.2 4.4 fusion.19
  136.7 1.5 fusion.25
  138.1 1.3 copy-done.2
  139.4 0.8 copy-done.6
  140.2 2.5 fusion.21
  142.8 3.4 fusion.23
  146.2 3.4 subtract_bitcast_fusion.1
  149.6 6.0 copy.33
  155.7 7.6 add_bitcast_fusion.1
  163.2 5.6 copy.32
  168.8 6.0 fusion.43
  174.8 5.6 convolution_subtract_fusion
  180.4 0.0 all-reduce.5.cloned.1.call-update
  180.5 0.0 copy-start.7
  180.5 0.0 reduce-scatter.5.cloned.1.call-start
  180.5 92.4 %all-reduce.5.cloned.1.call-done = f32[64,2,64,128]{3,0,2,1:T(8,128)} async-done(((f32[64,2,64,128]{3,0,2,1:T(8,128)}), f32[64,2,64,128]{3,0,2,1:T(8,128)}) %all-reduce.5.cloned.1.call-update) | async-done | bytes 4194320 | tf_op jit(solution)/shard_map/psum | solution.py:91
  272.9 2.7 convert_element_type.51
  275.6 1.3 copy-done.4
  277.0 1.6 fusion.122
  278.5 6.0 collective-permute-start
  284.5 1.3 collective-permute-start.1
  285.8 0.1 mul.185
  285.9 43.3 %collective-permute-done = bf16[64,1,64,128]{3,0,2,1:T(8,128)(2,1)} collective-permute-done((bf16[64,1,64,128]{3,0,2,1:T(8,128)(2,1)}, bf16[64,1,64,128]{3,0,2,1:T(8,128)(2,1)}, u32[]{:S(2)}, u32[]{:S(2)}) %collective-permute-start) | collective-permute-done | bytes 1048608 | tf_op jit(solution)/shard_map/ppermute | solution.py:17
  329.2 2.5 maximum_convert_fusion
  331.7 1.2 fusion.118
  332.9 0.2 fusion.121
  333.1 6.0 collective-permute-start.2
  339.1 1.3 collective-permute-start.3
  340.4 43.2 %collective-permute-done.2 = bf16[64,1,64,128]{3,0,2,1:T(8,128)(2,1)S(1)} collective-permute-done((bf16[64,1,64,128]{3,0,2,1:T(8,128)(2,1)S(1)}, bf16[64,1,64,128]{3,0,2,1:T(8,128)(2,1)S(1)}, u32[]{:S(2)}, u32[]{:S(2)}) %collective-permute-start.2) | collective-permute-done | bytes 1048608 | tf_op jit(solution)/shard_map/ppermute | solution.py:17
  383.6 0.7 maximum_convert_fusion.1
  384.3 1.1 fusion.10
  385.3 4.6 fusion.39
  390.0 4.4 fusion.36
  394.4 1.5 fusion.28
  395.9 1.5 fusion.24
  397.4 1.5 add_bitcast_fusion
  398.9 5.8 fusion
  404.7 1.6 subtract_bitcast_fusion
  406.3 5.6 fusion.16
  411.9 5.1 copy.38
  417.0 0.0 reduce-scatter.5.cloned.1.call-update
  417.0 382.3 %reduce-scatter.5.cloned.1.call-done = f32[1,150,128]{2,1,0:T(8,128)} async-done(((f32[64,150,128]{2,1,0:T(8,128)}), f32[1,150,128]{2,1,0:T(8,128)}) %reduce-scatter.5.cloned.1.call-update) | async-done | bytes 76816
  799.3 1.6 copy.39
  (16 shorter events, 0.0 us)
Async XLA Ops:
  6.5 125.7 %all-gather.2.cloned.1.call-start = ((), (), s32[]{:S(2)}) async-start(), calls=%async_computation.1 | async-start | bytes 2529280 | tf_op jit(solution)/shard_map/all_gather | solution.py:74
  7.3 265.7 %all-reduce.5.cloned.1.call-start = ((), (), s32[]{:S(2)}) async-start(), calls=%async_computation.2 | async-start | bytes 8388608 | tf_op jit(solution)/shard_map/psum | solution.py:91
  132.2 4.4 copy-start
  136.6 2.8 copy-start.2
  136.7 3.6 copy-start.6
  168.8 6.0 copy-start.3
  180.5 105.3 %copy-start.7 = (f32[128]{0:T(128)S(1)}, f32[128]{0:T(128)}, u32[]{:S(2)}) copy-start(f32[128]{0:T(128)} %param.5) | copy-start | bytes 1540
  180.5 618.9 %reduce-scatter.5.cloned.1.call-start = ((), (), s32[]{:S(2)}) async-start(), calls=%async_computation.3 | async-start | bytes 5058560
  275.6 1.4 copy-start.4
  278.5 50.7 %collective-permute-start = (bf16[64,1,64,128]{3,0,2,1:T(8,128)(2,1)}, bf16[64,1,64,128]{3,0,2,1:T(8,128)(2,1)}, u32[]{:S(2)}, u32[]{:S(2)}) collective-permute-start(bf16[64,1,64,128]{3,0,2,1:T(8,128)(2,1)} %get-tuple-element.11), channel_id=1, source_target_pairs={{0,4},{4,8},{8,12},{12,16},{16,20},{20,24},{24,28},{28,32},{32,36}... | collective-permute-start | bytes 3145736 | tf_op jit(solution)/shard_map/ppermute | solution.py:17
  284.5 44.7 %collective-permute-start.1 = (bf16[64,1,64,128]{3,0,2,1:T(8,128)(2,1)}, bf16[64,1,64,128]{3,0,2,1:T(8,128)(2,1)}, u32[]{:S(2)}, u32[]{:S(2)}) collective-permute-start(bf16[64,1,64,128]{3,0,2,1:T(8,128)(2,1)} %get-tuple-element.12), channel_id=1, source_target_pairs={{4,0},{8,4},{12,8},{16,12},{20,16},{24,20},{28,24},{32,28},{36,32}... | collective-permute-start | bytes 3145736 | tf_op jit(solution)/shard_map/ppermute | solution.py:20
  285.9 45.8 %copy-start.5 = (f32[64,2,64,128]{3,0,2,1:T(8,128)S(1)}, f32[64,2,64,128]{3,0,2,1:T(8,128)}, u32[]{:S(2)}) copy-start(f32[64,2,64,128]{3,0,2,1:T(8,128)} %all-reduce.5.cloned.1.call-done) | copy-start | bytes 12582916
  333.1 50.5 %collective-permute-start.2 = (bf16[64,1,64,128]{3,0,2,1:T(8,128)(2,1)S(1)}, bf16[64,1,64,128]{3,0,2,1:T(8,128)(2,1)S(1)}, u32[]{:S(2)}, u32[]{:S(2)}) collective-permute-start(bf16[64,1,64,128]{3,0,2,1:T(8,128)(2,1)S(1)} %get-tuple-element.9), channel_id=1, source_target_pairs={{0,4},{4,8},{8,12},{12,16},{16,20},{20,24},{24,28},{28,32},{32,36}... | collective-permute-start | bytes 3145736 | tf_op jit(solution)/shard_map/ppermute | solution.py:17
  339.1 44.5 %collective-permute-start.3 = (bf16[64,1,64,128]{3,0,2,1:T(8,128)(2,1)S(1)}, bf16[64,1,64,128]{3,0,2,1:T(8,128)(2,1)S(1)}, u32[]{:S(2)}, u32[]{:S(2)}) collective-permute-start(bf16[64,1,64,128]{3,0,2,1:T(8,128)(2,1)S(1)} %get-tuple-element.10), channel_id=1, source_target_pairs={{4,0},{8,4},{12,8},{16,12},{20,16},{24,20},{28,24},{32,28},{36,32}... | collective-permute-start | bytes 3145736 | tf_op jit(solution)/shard_map/ppermute | solution.py:20
  390.0 4.4 copy-start.1
Sparse Core Ops, SparseCore 0:
  10.8 121.3 all-gather.1
  180.6 92.2 all-reduce.4
  417.1 382.1 reduce-scatter.4
where the time goes:
time: 816 us; the launch traced here: 808 us
  waiting for transfers between devices  674 us (83%)
  matrix products  60.9 us (7%)
  local copies, waits for them, and re-layouts  36.4 us (4%)
  starting transfers between devices  14.6 us (2%)
  between operations  13.6 us (2%)
    unnamed x4, waiting for transfers between devices  383 us
    all_gather x1, waiting for transfers between devices, shards(): lax.all_gather(readings, 'param', axis=0, tiled=True)  112 us
    psum x1, waiting for transfers between devices, shards(): grid = lax.psum(grid, 'sensor')  92.4 us
    ppermute x2, waiting for transfers between devices, with_halo(): lax.ppermute(lax.slice_in_dim(block, block.shape[dim] - width, None, axis...  86.6 us
  transfers between devices with their start and end apart: 7, of which 5 were waited for; matrix products, arithmetic and copies ran while one was open for 2% of the time, Pallas kernels for 0%

commit v1 on v0

--- a/solution.py
+++ b/solution.py
@@ -1,3 +1,4 @@
+import functools
 import math
 import jax
 import jax.numpy as jnp
@@ -7,6 +8,19 @@
 STEPS = 64
 GY = 64
 NCOL = 128
+
+
+def begin_digits_on(block_in, lane_axis):
+    pile = []
+    for _ in range(lax.axis_size(lane_axis)):
+        pile.append(block_in)
+    e_now = jnp.stack(pile, 0)
+    arr_next = lax.all_to_all(e_now, axis_name=lane_axis, split_axis=0, concat_axis=0)
+    tile_out = jnp.concatenate(arr_next, 0)
+    return tile_out
+
+
+_link_corner = functools.partial(begin_digits_on, lane_axis="param")
 
 
 def with_halo(block, sides, width):
@@ -70,9 +84,7 @@
     points = spectra.shape[3]
     rows_here = points // GY
     empty_data = jnp.zeros((STEPS + 1, sens_rows, NCOL), jnp.float32)
-    data_re, data_im = accumulate(
-        (empty_data, empty_data), lax.all_gather(readings, "param", axis=0, tiled=True)
-    )
+    data_re, data_im = accumulate((empty_data, empty_data), _link_corner(readings))
     data_re = data_re.astype(jnp.bfloat16)
     data_im = data_im.astype(jnp.bfloat16)
     spectrum_real = spectra[0]

time: 816 us -> 769 us (0.942)
  waiting for transfers between devices: 674 us -> 607 us
  starting transfers between devices: 14.6 us -> 28.5 us
    all_gather x1 -> x0, waiting for transfers between devices: 112 us -> none  [shards(): lax.all_gather(readings, 'param', axis=0, tiled=True)]
    all_to_all x0 -> x1, waiting for transfers between devices: none -> 48.5 us  [begin_digits_on(): lax.all_to_all(e_now, axis_name=lane_axis, split_axis=0, concat_axis=0)]
    all_to_all x0 -> x1, starting transfers between devices: none -> 13.9 us  [begin_digits_on(): lax.all_to_all(e_now, axis_name=lane_axis, split_axis=0, concat_axis=0)]
    unnamed x4 -> x3, waiting for transfers between devices: 383 us -> 382 us
where the time goes in v1:
time: 769 us; the launch traced here: 760 us
  waiting for transfers between devices  607 us (79%)
  matrix products  63.8 us (8%)
  local copies, waits for them, and re-layouts  38.7 us (5%)
  starting transfers between devices  28.5 us (4%)
  between operations  14.1 us (2%)
  other arithmetic  8.24 us (1%)
    unnamed x3, waiting for transfers between devices  382 us
    psum x1, waiting for transfers between devices, shards(): grid = lax.psum(grid, 'sensor')  89.8 us
    ppermute x2, waiting for transfers between devices, with_halo(): lax.ppermute(lax.slice_in_dim(block, block.shape[dim] - width, None, axis...  86.6 us
    all_to_all x1, waiting for transfers between devices, begin_digits_on(): lax.all_to_all(e_now, axis_name=lane_axis, split_axis=0, concat_axis=0)  48.5 us
  transfers between devices with their start and end apart: 7, of which 5 were waited for; matrix products, arithmetic and copies ran while one was open for 2% of the time, Pallas kernels for 0%

profile of v1, /device:TPU:8, one launch (start us, length us, event | category | flops | bytes accessed | tf_op | source)
XLA Modules:
  0.0 759.8 jit_solution(13633857866862219203)
XLA Ops:
  6.5 2.6 stack.2
  9.1 13.9 %all-to-all-start = ((bf16[64,1,150,128]{3,2,1,0:T(8,128)(2,1)}), bf16[64,1,150,128]{3,2,1,0:T(8,128)(2,1)}, u32[]{:S(2)}, u32[]{:S(2)}) async-start(bf16[64,1,150,128]{3,2,1,0:T(8,128)(2,1)} %stack.2), calls=%async_computation | async-start | bytes 4980736 | tf_op jit(solution)/shard_map/all_to_all | solution.py:18
  23.0 0.0 all-reduce.5.cloned.1.call-start
  23.1 10.1 %fusion.122 = (bf16[1,65,150,128]{3,0,2,1:T(2,128)(2,1)S(1)}, bf16[1,65,150,128]{3,0,2,1:T(2,128)(2,1)S(1)}) fusion(bf16[2,65,150,128]{3,0,2,1:T(2,128)(2,1)} %param.4), kind=kLoop, calls=%fused_computation.128 | loop fusion | bytes 9984000 | tf_op jit(solution)/shard_map/slice | solution.py:91
  33.2 2.8 copy_bitcast_fusion
  36.0 48.5 %all-to-all-done = bf16[64,1,150,128]{3,2,1,0:T(8,128)(2,1)} async-done(((bf16[64,1,150,128]{3,2,1,0:T(8,128)(2,1)}), bf16[64,1,150,128]{3,2,1,0:T(8,128)(2,1)}, u32[]{:S(2)}, u32[]{:S(2)}) %all-to-all-start) | async-done | bytes 2457632 | tf_op jit(solution)/shard_map/all_to_all | solution.py:18
  84.4 4.4 fusion.16
  88.8 1.5 fusion.27
  90.3 0.9 copy-done.2
  91.2 4.2 fusion.18
  95.5 3.4 fusion.25
  98.9 3.4 subtract_bitcast_fusion.1
  102.3 6.0 copy.29
  108.4 7.6 add_bitcast_fusion.1
  116.0 5.6 copy.28
  121.6 6.0 fusion.45
  127.5 5.6 convolution_subtract_fusion
  133.2 0.0 all-reduce.5.cloned.1.call-update
  133.2 0.0 reduce-scatter.5.cloned.1.call-start
  133.2 89.8 %all-reduce.5.cloned.1.call-done = f32[64,2,64,128]{3,0,2,1:T(8,128)} async-done(((f32[64,2,64,128]{3,0,2,1:T(8,128)}), f32[64,2,64,128]{3,0,2,1:T(8,128)}) %all-reduce.5.cloned.1.call-update) | async-done | bytes 4194320 | tf_op jit(solution)/shard_map/psum | solution.py:103
  223.0 2.7 convert_element_type.51
  225.7 1.4 copy-done.5
  227.1 1.6 fusion.124
  228.6 6.0 collective-permute-start
  234.6 1.3 collective-permute-start.1
  235.9 0.1 mul.185
  236.0 43.3 %collective-permute-done = bf16[64,1,64,128]{3,0,2,1:T(8,128)(2,1)} collective-permute-done((bf16[64,1,64,128]{3,0,2,1:T(8,128)(2,1)}, bf16[64,1,64,128]{3,0,2,1:T(8,128)(2,1)}, u32[]{:S(2)}, u32[]{:S(2)}) %collective-permute-start) | collective-permute-done | bytes 1048608 | tf_op jit(solution)/shard_map/ppermute | solution.py:31
  279.3 2.5 maximum_convert_fusion
  281.8 1.2 fusion.120
  283.0 0.2 fusion.123
  283.2 6.0 collective-permute-start.2
  289.2 1.3 collective-permute-start.3
  290.5 43.2 %collective-permute-done.2 = bf16[64,1,64,128]{3,0,2,1:T(8,128)(2,1)S(1)} collective-permute-done((bf16[64,1,64,128]{3,0,2,1:T(8,128)(2,1)S(1)}, bf16[64,1,64,128]{3,0,2,1:T(8,128)(2,1)S(1)}, u32[]{:S(2)}, u32[]{:S(2)}) %collective-permute-start.2) | collective-permute-done | bytes 1048608 | tf_op jit(solution)/shard_map/ppermute | solution.py:31
  333.7 0.8 maximum_convert_fusion.1
  334.6 1.1 fusion.10
  335.6 4.4 fusion.41
  340.1 4.4 fusion.38
  344.5 1.5 fusion.30
  346.0 1.5 fusion.26
  347.4 1.5 add_bitcast_fusion
  349.0 7.3 fusion
  356.3 1.6 subtract_bitcast_fusion
  357.8 0.8 copy-done.3
  358.7 5.6 fusion.20
  364.2 5.1 copy.34
  369.3 0.0 reduce-scatter.5.cloned.1.call-update
  369.3 381.7 %reduce-scatter.5.cloned.1.call-done = f32[1,150,128]{2,1,0:T(8,128)} async-done(((f32[64,150,128]{2,1,0:T(8,128)}), f32[1,150,128]{2,1,0:T(8,128)}) %reduce-scatter.5.cloned.1.call-update) | async-done | bytes 76816
  751.0 1.6 copy.35
  (16 shorter events, 0.0 us)
Async XLA Ops:
  9.1 75.3 %all-to-all-start = ((bf16[64,1,150,128]{3,2,1,0:T(8,128)(2,1)}), bf16[64,1,150,128]{3,2,1,0:T(8,128)(2,1)}, u32[]{:S(2)}, u32[]{:S(2)}) async-start(bf16[64,1,150,128]{3,2,1,0:T(8,128)(2,1)} %stack.2), calls=%async_computation | async-start | bytes 4980736 | tf_op jit(solution)/shard_map/all_to_all | solution.py:18
  23.0 200.0 %all-reduce.5.cloned.1.call-start = ((), (), s32[]{:S(2)}) async-start(), calls=%async_computation.2 | async-start | bytes 8388608 | tf_op jit(solution)/shard_map/psum | solution.py:103
  84.4 4.4 copy-start
  88.8 2.4 copy-start.2
  121.6 6.0 copy-start.4
  133.2 102.7 %copy-start.7 = (f32[128]{0:T(128)S(1)}, f32[128]{0:T(128)}, u32[]{:S(2)}) copy-start(f32[128]{0:T(128)} %param.5) | copy-start | bytes 1540
  133.2 617.8 %reduce-scatter.5.cloned.1.call-start = ((), (), s32[]{:S(2)}) async-start(), calls=%async_computation.3 | async-start | bytes 5058560
  225.7 1.4 copy-start.5
  228.6 50.7 %collective-permute-start = (bf16[64,1,64,128]{3,0,2,1:T(8,128)(2,1)}, bf16[64,1,64,128]{3,0,2,1:T(8,128)(2,1)}, u32[]{:S(2)}, u32[]{:S(2)}) collective-permute-start(bf16[64,1,64,128]{3,0,2,1:T(8,128)(2,1)} %get-tuple-element.11), channel_id=1, source_target_pairs={{0,4},{4,8},{8,12},{12,16},{16,20},{20,24},{24,28},{28,32},{32,36}... | collective-permute-start | bytes 3145736 | tf_op jit(solution)/shard_map/ppermute | solution.py:31
  234.6 44.7 %collective-permute-start.1 = (bf16[64,1,64,128]{3,0,2,1:T(8,128)(2,1)}, bf16[64,1,64,128]{3,0,2,1:T(8,128)(2,1)}, u32[]{:S(2)}, u32[]{:S(2)}) collective-permute-start(bf16[64,1,64,128]{3,0,2,1:T(8,128)(2,1)} %get-tuple-element.12), channel_id=1, source_target_pairs={{4,0},{8,4},{12,8},{16,12},{20,16},{24,20},{28,24},{32,28},{36,32}... | collective-permute-start | bytes 3145736 | tf_op jit(solution)/shard_map/ppermute | solution.py:34
  236.0 45.8 %copy-start.6 = (f32[64,2,64,128]{3,0,2,1:T(8,128)S(1)}, f32[64,2,64,128]{3,0,2,1:T(8,128)}, u32[]{:S(2)}) copy-start(f32[64,2,64,128]{3,0,2,1:T(8,128)} %all-reduce.5.cloned.1.call-done) | copy-start | bytes 12582916
  283.2 50.5 %collective-permute-start.2 = (bf16[64,1,64,128]{3,0,2,1:T(8,128)(2,1)S(1)}, bf16[64,1,64,128]{3,0,2,1:T(8,128)(2,1)S(1)}, u32[]{:S(2)}, u32[]{:S(2)}) collective-permute-start(bf16[64,1,64,128]{3,0,2,1:T(8,128)(2,1)S(1)} %get-tuple-element.9), channel_id=1, source_target_pairs={{0,4},{4,8},{8,12},{12,16},{16,20},{20,24},{24,28},{28,32},{32,36}... | collective-permute-start | bytes 3145736 | tf_op jit(solution)/shard_map/ppermute | solution.py:31
  289.2 44.5 %collective-permute-start.3 = (bf16[64,1,64,128]{3,0,2,1:T(8,128)(2,1)S(1)}, bf16[64,1,64,128]{3,0,2,1:T(8,128)(2,1)S(1)}, u32[]{:S(2)}, u32[]{:S(2)}) collective-permute-start(bf16[64,1,64,128]{3,0,2,1:T(8,128)(2,1)S(1)} %get-tuple-element.10), channel_id=1, source_target_pairs={{4,0},{8,4},{12,8},{16,12},{20,16},{24,20},{28,24},{32,28},{36,32}... | collective-permute-start | bytes 3145736 | tf_op jit(solution)/shard_map/ppermute | solution.py:34
  340.1 4.4 copy-start.1
  356.3 2.4 copy-start.3
Sparse Core Ops, SparseCore 0:
  133.3 89.6 all-reduce.4
  369.4 381.5 reduce-scatter.4
